TPU v7x, 512 devices: a whole 4x4x16 slice. The times are simulated.
512 devices in a mesh: dp: 32 (over z, core), expert: 16 (over x, y).
Axes of the slice: x: 4, y: 4, z: 16, core: 2. Of those that a mesh axis runs over, the one named last changes fastest.
Arguments:
- cached_hidden: bfloat16 [65536, 1536], P(('dp', 'expert')), may hold values from -6 to 6
- direction: bfloat16 [16, 2880, 1536], P('expert', 'dp'), may hold values from -1 to 1
- expert_ids: int32 [65536, 4], P(('dp', 'expert')), may hold values from 0 to 127, as said below
- gate_weights: float32 [65536, 4], P(('dp', 'expert')), may hold values from 0.05 to 1
Outputs:
- curvature_product: float32 [16, 2880, 1536], P('expert', 'dp')
Inputs may be any that keep to these rules, and one draw needn't show every extreme that they name: `expert_ids`: each row names 4 different experts, at most two of them below 16. Among the 128 rows of one device no expert below 16 is named more than 8 times; for every dp index, some expert below 16 is named exactly 8 times by the rows of each device with that dp index.
All inputs are finite; a program needn't handle non-finite values.
Results may differ from a plain program's by a relative error of at most 0.0034.
Values may be sent and summed in bfloat16 or wider, within the bound.
No kernel may reach another device: no remote copies, remote signals or barrier semaphores. Data moves between devices by JAX's collectives and lax.ppermute only.
A program may use at most 128 MiB of HBM per device.

v0:
```python
import math
import jax
import jax.numpy as jnp
from jax import lax
from jax.sharding import PartitionSpec as P


def slot_positions(block_ids, experts):
    flat = block_ids.reshape(-1)
    onehot = (flat[:, None] == jnp.arange(experts, dtype=jnp.int32)[None, :]).astype(jnp.int32)
    before = jnp.cumsum(onehot, axis=0) - onehot
    return jnp.sum(before * onehot, axis=1).reshape(block_ids.shape)


def body(cached_hidden, direction, expert_ids, gate_weights):
    dp_count = lax.axis_size("dp")
    owner_count = lax.axis_size("expert")
    slot_rows = cached_hidden.shape[0]
    capacity = slot_rows // owner_count
    tok_count = expert_ids.shape[0]
    width = direction.shape[1] * dp_count
    local_dir = direction[0]
    rows_all = lax.all_gather(cached_hidden, "dp", axis=0, tiled=True)
    tangent = lax.dot_general(
        rows_all, local_dir, (((1,), (1,)), ((), ())), preferred_element_type=jnp.float32
    )
    tangent = tangent.astype(jnp.bfloat16).reshape(
        dp_count, owner_count, capacity, local_dir.shape[0]
    )
    returned = lax.all_to_all(
        lax.all_to_all(tangent, "dp", split_axis=0, concat_axis=3, tiled=True),
        "expert",
        split_axis=1,
        concat_axis=1,
        tiled=True,
    )
    flat_rows = returned.reshape(owner_count * capacity, width)
    treated = expert_ids < owner_count
    slot_pos = slot_positions(expert_ids, owner_count)
    target = expert_ids * capacity + slot_pos
    lookup = jnp.where(treated, target, 0).reshape(-1)
    dropped = jnp.where(treated, target, owner_count * capacity).reshape(-1)
    gates = jnp.where(treated, gate_weights, 0.0)
    picked = jnp.take(flat_rows, lookup, axis=0).reshape(tok_count, expert_ids.shape[1], width)
    scale_factor = 1.0 / math.sqrt(tok_count * dp_count * owner_count)
    combined = jnp.sum(gates[..., None] * picked.astype(jnp.float32), axis=1) * scale_factor
    outgoing = (gates[..., None] * combined[:, None, :]).astype(jnp.bfloat16)
    buffer = jnp.zeros((owner_count * capacity, width), jnp.bfloat16)
    buffer = buffer.at[dropped].set(outgoing.reshape(-1, width), mode="drop")
    buffer = buffer.reshape(1, owner_count, capacity, width)
    arrived = lax.all_to_all(buffer, "expert", split_axis=1, concat_axis=1, tiled=True)
    adjoint = lax.all_to_all(arrived, "dp", split_axis=3, concat_axis=0, tiled=True)
    adjoint_rows = adjoint.reshape(-1, adjoint.shape[3])
    gradient = lax.dot_general(
        adjoint_rows, rows_all, (((0,), (0,)), ((), ())), preferred_element_type=jnp.float32
    )
    return gradient.reshape(1, gradient.shape[0], gradient.shape[1])


def solution(mesh):
    return jax.shard_map(
        body,
        mesh=mesh,
        in_specs=(
            P(("dp", "expert"), None),
            P("expert", "dp", None),
            P(("dp", "expert"), None),
            P(("dp", "expert"), None),
        ),
        out_specs=P("expert", "dp", None),
        check_vma=False,
    )
```

profile of v0, /device:TPU:1, one launch (start us, length us, event | category | flops | bytes accessed | tf_op | source)
XLA Modules:
  0.0 336.8 jit_solution(6748889101096679168)
XLA Ops:
  6.5 0.0 copy-start
  6.5 0.0 all-gather.2.cloned.1.call-start
  6.5 0.7 all-gather.2.cloned.1.call-update
  7.3 95.0 %all-gather.2.cloned.1.call-done = bf16[4096,1536]{1,0:T(8,128)(2,1)} async-done(((bf16[128,1536]{1,0:T(8,128)(2,1)}), bf16[4096,1536]{1,0:T(8,128)(2,1)}) %all-gather.2.cloned.1.call-update) | async-done | bytes 12582928 | tf_op jit(solution)/shard_map/all_gather | solution.py:23
  102.3 0.0 copy-done
  102.3 8.5 %convolution_convert_fusion = bf16[4096,90]{0,1:T(8,128)(2,1)S(1)} fusion(bf16[4096,1536]{1,0:T(8,128)(2,1)} %all-gather.2.cloned.1.call-done, bf16[1,90,1536]{2,1,0:T(8,128)(2,1)S(1)} %copy-done), kind=kOutput, calls=%fused_computation.4 | convolution fusion | flops 1132830720 | bytes 13596672 | tf_op jit(solution)/shard_map/dot_general | solution.py:24
  110.7 0.0 copy-start.1
  110.7 0.0 copy-start.2
  110.8 1.4 copy.65
  112.2 7.8 %all-to-all-start = ((bf16[32,16,8,90]{3,2,1,0:T(8,128)(2,1)}), bf16[32,16,8,90]{3,2,1,0:T(8,128)(2,1)S(1)}, u32[]{:S(2)}, u32[]{:S(2)}) async-start(bf16[32,16,8,90]{3,2,1,0:T(8,128)(2,1)} %bitcast.3), calls=%async_computation | async-start | bytes 2097152 | tf_op jit(solution)/shard_map/all_to_all | solution.py:31
  120.0 0.0 copy-done.1
  120.0 0.1 copy.57
  120.1 0.1 eq.29
  120.2 0.1 eq.25
  120.3 0.0 copy-done.2
  120.4 0.1 copy.62
  120.5 0.1 mul.48
  120.6 1.2 reduce-window.6
  121.7 0.2 slice_reduce_fusion
  122.0 0.1 fusion.6
  122.1 0.1 reshape.119
  122.2 0.1 copy.60
  122.3 0.1 copy.64
  122.5 53.2 %all-to-all-done = bf16[32,16,8,90]{3,2,1,0:T(8,128)(2,1)S(1)} async-done(((bf16[32,16,8,90]{3,2,1,0:T(8,128)(2,1)}), bf16[32,16,8,90]{3,2,1,0:T(8,128)(2,1)S(1)}, u32[]{:S(2)}, u32[]{:S(2)}) %all-to-all-start) | async-done | bytes 737312 | tf_op jit(solution)/shard_map/all_to_all | solution.py:31
  175.7 0.7 copy.66
  176.4 2.9 all_to_all.33
  179.3 6.5 %all-to-all-start.1 = ((bf16[1,16,8,2880]{3,2,0,1:T(8,128)(2,1)}), bf16[1,16,8,2880]{3,2,0,1:T(8,128)(2,1)S(1)}, u32[]{:S(2)}, u32[]{:S(2)}) async-start(bf16[1,16,8,2880]{3,2,0,1:T(8,128)(2,1)} %bitcast.6), calls=%async_computation.1 | async-start | bytes 1507328 | tf_op jit(solution)/shard_map/all_to_all | solution.py:30
  185.8 0.1 copy.61
  185.9 0.1 reshape.120
  186.0 0.1 copy.68
  186.1 0.1 reshape.123
  186.3 11.9 %all-to-all-done.1 = bf16[1,16,8,2880]{3,2,0,1:T(8,128)(2,1)S(1)} async-done(((bf16[1,16,8,2880]{3,2,0,1:T(8,128)(2,1)}), bf16[1,16,8,2880]{3,2,0,1:T(8,128)(2,1)S(1)}, u32[]{:S(2)}, u32[]{:S(2)}) %all-to-all-start.1) | async-done | bytes 737312 | tf_op jit(solution)/shard_map/all_to_all | solution.py:30
  198.2 3.7 %gather_fusion = bf16[512,2880]{1,0:T(8,128)(2,1)} fusion(bf16[128,2880]{1,0:T(8,128)(2,1)S(1)} %bitcast.44, s32[1024]{0:T(1024)S(1)} %pad_clamp_fusion), kind=kCustom, calls=%fused_computation | custom fusion | bytes 5900288 | tf_op jit(solution)/shard_map/jit(_take)/gather | solution.py:44
  201.9 4.7 %gather.7 = bf16[128,4,2880]{2,1,0:T(4,128)(2,1)S(1)} reshape(bf16[512,2880]{1,0:T(8,128)(2,1)} %gather_fusion) | data formatting | bytes 5898240 | tf_op jit(solution)/shard_map/jit(_take)/gather | solution.py:44
  206.6 6.3 %multiply_reduce_fusion = f32[128,2880]{1,0:T(8,128)S(1)} fusion(bf16[128,4,2880]{2,1,0:T(4,128)(2,1)S(1)} %gather.7, f32[128,4]{1,0:T(8,128)S(1)} %copy.62, pred[128,4]{1,0:T(8,128)(4,1)S(1)} %copy.64), kind=kLoop, calls=%fused_computation.3 | loop fusion | flops 5529600 | bytes 4426240 | tf_op jit(solution)/shard_map/reduce_sum | solution.py:46
  212.9 0.1 broadcast_multiply_fusion
  213.0 3.6 %mul.54 = f32[128,4,2880]{2,1,0:T(4,128)} broadcast(f32[128,2880]{1,0:T(8,128)S(1)} %broadcast_multiply_fusion), dimensions={0,2} | broadcast | bytes 7372800 | tf_op jit(solution)/shard_map/mul | solution.py:47
  216.5 7.7 %mul.55 = f32[512,2880]{1,0:T(8,128)} reshape(f32[128,4,2880]{2,1,0:T(4,128)} %mul.54) | data formatting | bytes 11796480 | tf_op jit(solution)/shard_map/mul | solution.py:47
  224.3 7.1 %scatter_custom_fusion = bf16[128,2880]{1,0:T(8,128)(2,1)S(1)} fusion(s32[512]{0:T(512)S(1)} %bitcast.52, f32[512,2880]{1,0:T(8,128)} %mul.55, f32[512]{0:T(512)S(1)} %mul.48, bf16[]{:T(256)} %constant.9.clone.1), kind=kCustom, calls=%fused_computation.5 | custom fusion | flops 2949120 | bytes 6637570 | tf_op jit(solution)/shard_map/scatter | solution.py:49
  231.4 15.4 %all_to_all.43 = bf16[1,16,8,2880]{3,2,0,1:T(8,128)(2,1)S(1)} all-to-all(bf16[1,16,8,2880]{3,2,0,1:T(8,128)(2,1)S(1)} %bitcast.50), channel_id=1, replica_groups=mesh['dp'=32,'expert'=16] {'expert'}, dimensions={1} | all-to-all | bytes 1474560 | tf_op jit(solution)/shard_map/all_to_all | solution.py:51
  246.8 5.5 %copy.69 = bf16[1,16,8,2880]{1,2,0,3:T(8,128)(2,1)} copy(bf16[1,16,8,2880]{3,2,0,1:T(8,128)(2,1)S(1)} %all_to_all.43) | data formatting | bytes 1474560 | tf_op jit(solution)/shard_map/all_to_all | solution.py:51
  252.4 8.5 %reshape.146 = bf16[32,2,5760]{2,1,0:T(2,128)(2,1)S(1)} reshape(bf16[2880,1,8,16]{3,2,1,0:T(8,128)(2,1)} %bitcast.45) | data formatting | bytes 1474560
  260.9 48.5 %all_to_all.44 = bf16[32,2,5760]{2,1,0:T(2,128)(2,1)S(1)} all-to-all(bf16[32,2,5760]{2,1,0:T(2,128)(2,1)S(1)} %reshape.146), channel_id=1, replica_groups=mesh['dp'=32,'expert'=16] {'dp'}, dimensions={0} | all-to-all | bytes 1474560 | tf_op jit(solution)/shard_map/all_to_all | solution.py:52
  309.4 5.5 %reshape.147 = bf16[2880,1,8,16]{3,2,1,0:T(8,128)(2,1)} reshape(bf16[32,2,5760]{2,1,0:T(2,128)(2,1)S(1)} %all_to_all.44) | data formatting | bytes 1474560
  314.9 6.5 %copy.73 = bf16[1,16,8,32,90]{4,3,2,1,0:T(8,128)(2,1)S(1)} copy(bf16[1,16,8,32,90]{1,2,4,3,0:T(8,128)(2,1)} %bitcast.46) | data formatting | bytes 1474560 | tf_op jit(solution)/shard_map/all_to_all | solution.py:52
  321.4 0.4 copy.71
  321.9 6.7 %convolution_bitcast_fusion = f32[1,90,1536]{2,1,0:T(8,128)S(1)} fusion(bf16[4096,90]{1,0:T(8,128)(2,1)S(1)} %bitcast.47, bf16[4096,1536]{1,0:T(8,128)(2,1)} %all-gather.2.cloned.1.call-done), kind=kOutput, calls=%fused_computation.7 | convolution fusion | flops 1132462080 | bytes 13873152 | tf_op jit(solution)/shard_map/dot_general | solution.py:54
  328.6 1.4 copy.72
  (9 shorter events, 0.1 us)
Async XLA Ops:
  6.5 95.7 %copy-start = (bf16[1,90,1536]{2,1,0:T(8,128)(2,1)S(1)}, bf16[1,90,1536]{2,1,0:T(8,128)(2,1)}, u32[]{:S(2)}) copy-start(bf16[1,90,1536]{2,1,0:T(8,128)(2,1)} %param.5) | copy-start | bytes 829444
  6.5 95.7 %all-gather.2.cloned.1.call-start = ((), (), s32[]{:S(2)}) async-start(), calls=%async_computation.4 | async-start | bytes 12976128 | tf_op jit(solution)/shard_map/all_gather | solution.py:23
  110.7 9.3 %copy-start.1 = (s32[128,4]{0,1:T(4,128)S(1)}, s32[128,4]{0,1:T(4,128)}, u32[]{:S(2)}) copy-start(s32[128,4]{0,1:T(4,128)} %param.6) | copy-start | bytes 6148
  110.7 9.6 %copy-start.2 = (f32[128,4]{0,1:T(4,128)S(1)}, f32[128,4]{0,1:T(4,128)}, u32[]{:S(2)}) copy-start(f32[128,4]{0,1:T(4,128)} %param.7) | copy-start | bytes 6148
  112.2 63.5 %all-to-all-start = ((bf16[32,16,8,90]{3,2,1,0:T(8,128)(2,1)}), bf16[32,16,8,90]{3,2,1,0:T(8,128)(2,1)S(1)}, u32[]{:S(2)}, u32[]{:S(2)}) async-start(bf16[32,16,8,90]{3,2,1,0:T(8,128)(2,1)} %bitcast.3), calls=%async_computation | async-start | bytes 2097152 | tf_op jit(solution)/shard_map/all_to_all | solution.py:31
  179.3 19.0 %all-to-all-start.1 = ((bf16[1,16,8,2880]{3,2,0,1:T(8,128)(2,1)}), bf16[1,16,8,2880]{3,2,0,1:T(8,128)(2,1)S(1)}, u32[]{:S(2)}, u32[]{:S(2)}) async-start(bf16[1,16,8,2880]{3,2,0,1:T(8,128)(2,1)} %bitcast.6), calls=%async_computation.1 | async-start | bytes 1507328 | tf_op jit(solution)/shard_map/all_to_all | solution.py:30
Sparse Core Ops, SparseCore 0:
  9.5 92.7 all-gather.1
where the time goes:
time: 338 us; the launch traced here: 337 us
  waiting for transfers between devices  161 us (48%)
  blocking collectives  63.9 us (19%)
  local copies, waits for them, and re-layouts  54 us (16%)
  matrix products  15.2 us (4%)
  other arithmetic  14.9 us (4%)
  starting transfers between devices  14.3 us (4%)
  between operations  13.6 us (4%)
    all_gather x1, waiting for transfers between devices, body(): rows_all = lax.all_gather(cached_hidden, 'dp', axis=0, tiled=True)  95 us
    all_to_all x1, waiting for transfers between devices, body(): lax.all_to_all(tangent, 'dp', split_axis=0, concat_axis=3, tiled=True)  53.2 us
    all_to_all x1, blocking collectives, body(): lax.all_to_all(arrived, 'dp', split_axis=3, concat_axis=0, tiled=True)  48.5 us
    all_to_all x1, blocking collectives, body(): lax.all_to_all(buffer, 'expert', split_axis=1, concat_axis=1, tiled=True)  15.4 us
    unnamed x9, local copies, waits for them, and re-layouts  14.2 us
    all_to_all x1, waiting for transfers between devices, body(): lax.all_to_all(lax.all_to_all(tangent, 'dp', split_axis=0, concat_axis=3,...  11.9 us
    mul x3, local copies, waits for them, and re-layouts, body(): outgoing = (gates[..., None] * combined[:, None, :]).astype(jnp.bfloat16)  11.4 us
    dot_general x1, matrix products, body(): lax.dot_general(rows_all, local_dir, (((1,), (1,)), ((), ())), preferred_...  8.46 us
  transfers between devices with their start and end apart: 3, of which 3 were waited for; matrix products, arithmetic and copies ran while one was open for 1% of the time, Pallas kernels for 0%

commit v1 on v0

--- a/solution.py
+++ b/solution.py
@@ -20,7 +20,9 @@
     tok_count = expert_ids.shape[0]
     width = direction.shape[1] * dp_count
     local_dir = direction[0]
-    rows_all = lax.all_gather(cached_hidden, "dp", axis=0, tiled=True)
+    rows_all = jnp.concatenate(
+        lax.all_to_all(jnp.stack([cached_hidden] * lax.axis_size("dp")), "dp", 0, 0), axis=0
+    )
     tangent = lax.dot_general(
         rows_all, local_dir, (((1,), (1,)), ((), ())), preferred_element_type=jnp.float32
     )

time: 338 us -> 799 us (2.36)
  blocking collectives: 63.9 us -> 631 us
  waiting for transfers between devices: 161 us -> 65.3 us
  between operations: 13.6 us -> 0.2 us
  local copies, waits for them, and re-layouts: 54 us -> 65.6 us
    all_to_all x0 -> x1, blocking collectives: none -> 567 us  [body(): lax.all_to_all(jnp.stack([cached_hidden] * lax.axis_size('dp')), 'dp', 0, 0)]
    all_gather x1 -> x0, waiting for transfers between devices: 95 us -> none  [body(): rows_all = lax.all_gather(cached_hidden, 'dp', axis=0, tiled=True)]
    unnamed x9 -> x13, local copies, waits for them, and re-layouts: 14.2 us -> 18.7 us
  transfers between devices with their start and end apart: 3 -> 2, of which waited for: 3 -> 2; matrix products, arithmetic and copies ran while one was open for 1% -> 0% of each run, Pallas kernels for 0% -> 0%
where the time goes in v1:
time: 799 us; the launch traced here: 798 us
  blocking collectives  631 us (79%)
  local copies, waits for them, and re-layouts  65.6 us (8%)
  waiting for transfers between devices  65.3 us (8%)
  other arithmetic  14.9 us (2%)
  starting transfers between devices  10.9 us (1%)
  matrix products  10.7 us (1%)
    all_to_all x1, blocking collectives, body(): lax.all_to_all(jnp.stack([cached_hidden] * lax.axis_size('dp')), 'dp', 0, 0)  567 us
    all_to_all x1, waiting for transfers between devices, body(): lax.all_to_all(tangent, 'dp', split_axis=0, concat_axis=3, tiled=True)  53.2 us
    all_to_all x1, blocking collectives, body(): lax.all_to_all(arrived, 'dp', split_axis=3, concat_axis=0, tiled=True)  49.2 us
    unnamed x13, local copies, waits for them, and re-layouts  18.7 us
  transfers between devices with their start and end apart: 2, of which 2 were waited for; matrix products, arithmetic and copies ran while one was open for 0% of the time, Pallas kernels for 0%

profile of v1, /device:TPU:1, one launch (start us, length us, event | category | flops | bytes accessed | tf_op | source)
XLA Modules:
  0.0 798.3 jit_solution(13873935513218160869)
XLA Ops:
  0.0 0.0 copy-start
  0.0 7.0 stack.2
  7.0 566.8 %all_to_all.48 = bf16[32,128,1536]{2,1,0:T(8,128)(2,1)S(1)} all-to-all(bf16[32,128,1536]{2,1,0:T(8,128)(2,1)} %stack.2), channel_id=1, replica_groups=mesh['dp'=32,'expert'=16] {'dp'}, dimensions={0} | all-to-all | bytes 25165824 | tf_op jit(solution)/shard_map/all_to_all | solution.py:24
  573.8 0.0 copy-start.2
  573.8 4.6 copy-done.2
  578.4 0.0 copy-done
  578.4 3.9 convolution_convert_fusion
  582.3 0.0 copy-start.3
  582.3 1.4 copy.65
  583.7 4.1 all-to-all-start.1
  587.8 0.0 copy-done.3
  587.8 0.1 copy.57
  587.9 0.1 eq.25
  588.0 0.1 eq.29
  588.2 0.0 copy-start.4
  588.2 1.2 reduce-window.6
  589.3 0.2 slice_reduce_fusion
  589.6 0.1 fusion.6
  589.7 0.1 reshape.124
  589.8 0.1 copy.60
  589.9 0.1 copy.61
  590.0 0.1 reshape.125
  590.1 0.1 copy.68
  590.3 0.1 reshape.129
  590.4 53.2 %all-to-all-done.1 = bf16[32,16,8,90]{3,2,1,0:T(8,128)(2,1)S(1)} async-done(((bf16[32,16,8,90]{3,2,1,0:T(8,128)(2,1)}), bf16[32,16,8,90]{3,2,1,0:T(8,128)(2,1)S(1)}, u32[]{:S(2)}, u32[]{:S(2)}) %all-to-all-start.1) | async-done | bytes 737312 | tf_op jit(solution)/shard_map/all_to_all | solution.py:33
  643.6 0.7 copy.66
  644.3 2.9 all_to_all.37
  647.1 6.8 all-to-all-start.2
  653.9 0.0 copy-done.4
  653.9 0.1 copy.62
  654.1 0.1 copy.64
  654.2 0.1 mul.48
  654.3 12.1 %all-to-all-done.2 = bf16[1,16,8,2880]{3,2,0,1:T(8,128)(2,1)S(1)} async-done(((bf16[1,16,8,2880]{3,2,0,1:T(8,128)(2,1)}), bf16[1,16,8,2880]{3,2,0,1:T(8,128)(2,1)S(1)}, u32[]{:S(2)}, u32[]{:S(2)}) %all-to-all-start.2) | async-done | bytes 737312 | tf_op jit(solution)/shard_map/all_to_all | solution.py:32
  666.4 3.7 gather_fusion
  670.1 4.7 gather.7
  674.8 6.3 multiply_reduce_fusion
  681.1 0.1 broadcast_multiply_fusion
  681.2 3.6 mul.54
  684.7 7.7 mul.55
  692.5 7.1 scatter_custom_fusion
  699.6 14.8 %all_to_all.49 = bf16[1,16,8,2880]{3,2,0,1:T(8,128)(2,1)S(1)} all-to-all(bf16[1,16,8,2880]{3,2,0,1:T(8,128)(2,1)S(1)} %bitcast.52), channel_id=1, replica_groups=mesh['dp'=32,'expert'=16] {'expert'}, dimensions={1} | all-to-all | bytes 1474560 | tf_op jit(solution)/shard_map/all_to_all | solution.py:53
  714.5 5.5 copy.69
  720.0 8.5 %reshape.152 = bf16[32,2,5760]{2,1,0:T(2,128)(2,1)S(1)} reshape(bf16[2880,1,8,16]{3,2,1,0:T(8,128)(2,1)} %bitcast.47) | data formatting | bytes 1474560
  728.5 49.2 %all_to_all.50 = bf16[32,2,5760]{2,1,0:T(2,128)(2,1)S(1)} all-to-all(bf16[32,2,5760]{2,1,0:T(2,128)(2,1)S(1)} %reshape.152), channel_id=1, replica_groups=mesh['dp'=32,'expert'=16] {'dp'}, dimensions={0} | all-to-all | bytes 1474560 | tf_op jit(solution)/shard_map/all_to_all | solution.py:54
  777.7 5.5 reshape.153
  783.2 6.5 copy.73
  789.7 0.4 copy.71
  790.2 0.0 copy-start.1
  790.2 6.8 convolution_bitcast_fusion
  797.0 1.4 copy.72
  798.3 0.0 copy-done.1
  (9 shorter events, 0.1 us)
Async XLA Ops:
  0.0 578.4 %copy-start = (bf16[1,90,1536]{2,1,0:T(8,128)(2,1)S(1)}, bf16[1,90,1536]{2,1,0:T(8,128)(2,1)}, u32[]{:S(2)}) copy-start(bf16[1,90,1536]{2,1,0:T(8,128)(2,1)} %param.5) | copy-start | bytes 829444
  573.8 4.6 copy-start.2
  582.3 5.5 copy-start.3
  583.7 59.9 %all-to-all-start.1 = ((bf16[32,16,8,90]{3,2,1,0:T(8,128)(2,1)}), bf16[32,16,8,90]{3,2,1,0:T(8,128)(2,1)S(1)}, u32[]{:S(2)}, u32[]{:S(2)}) async-start(bf16[32,16,8,90]{3,2,1,0:T(8,128)(2,1)} %bitcast.4), calls=%async_computation.1 | async-start | bytes 2097152 | tf_op jit(solution)/shard_map/all_to_all | solution.py:33
  588.2 65.8 %copy-start.4 = (f32[128,4]{0,1:T(4,128)S(1)}, f32[128,4]{0,1:T(4,128)}, u32[]{:S(2)}) copy-start(f32[128,4]{0,1:T(4,128)} %param.7) | copy-start | bytes 6148
  647.1 19.3 %all-to-all-start.2 = ((bf16[1,16,8,2880]{3,2,0,1:T(8,128)(2,1)}), bf16[1,16,8,2880]{3,2,0,1:T(8,128)(2,1)S(1)}, u32[]{:S(2)}, u32[]{:S(2)}) async-start(bf16[1,16,8,2880]{3,2,0,1:T(8,128)(2,1)} %bitcast.7), calls=%async_computation.2 | async-start | bytes 1507328 | tf_op jit(solution)/shard_map/all_to_all | solution.py:32
  790.2 8.2 %copy-start.1 = (bf16[1,90,1536]{2,1,0:T(8,128)(2,1)S(1)}, bf16[1,90,1536]{2,1,0:T(8,128)(2,1)}, u32[]{:S(2)}) copy-start(bf16[1,90,1536]{2,1,0:T(8,128)(2,1)} %param.5) | copy-start | bytes 829444
